TPU v7x, 32 devices: a whole 2x2x4 slice. The times are simulated.
32 devices in a mesh: frow: 4 (over x, core), fcol: 8 (over z, y).
Axes of the slice: x: 2, y: 2, z: 4, core: 2. Of those that a mesh axis runs over, the one named last changes fastest.
Arguments:
- facet_image: bfloat16 [2048, 4096], P('frow', 'fcol'), may hold values from -6 to 6
- row_offsets: int32 [2], replicated, may hold values from 0 to 65280
- col_offsets: int32 [2], replicated, may hold values from 0 to 65280
- vis_subgrid: int32 [16384], P(('frow', 'fcol')), may hold values from 0 to 3
- vis_u: int32 [16384], P(('frow', 'fcol')), may hold values from 0 to 255
- vis_v: int32 [16384], P(('frow', 'fcol')), may hold values from 0 to 255
- observed: float32 [2, 16384], P(None, ('frow', 'fcol')), may hold values from -6 to 6
Outputs:
- facet_residual: float32 [2048, 4096], P('frow', 'fcol')
- residual_vis: float32 [2, 16384], P(None, ('frow', 'fcol'))
Inputs may be any that keep to these rules, and one draw needn't show every extreme that they name: `vis_subgrid`: subgrid numbers count row by row over the 2 x 2 subgrids.
All inputs are finite; a program needn't handle non-finite values.
Results may differ from a plain program's by a relative error of at most 0.023.
Values may be sent and summed in bfloat16 or wider, within the bound.
A program may use at most 64 MiB of HBM per device.

v0:
```python
import math
import jax
import jax.numpy as jnp
from jax import lax
from jax.sharding import PartitionSpec as P

SKY = 65536
SG = 256
NR = 2
NC = 2


def wrapped(frequency, position):
    high_part = frequency // 256
    low_part = frequency % 256
    return (high_part * (position * 256 % SKY) + low_part * position) % SKY


def sky_tables(start, positions):
    frequency = start + jnp.arange(SG, dtype=jnp.int32)[:, None]
    angles = wrapped(frequency, positions[None, :]).astype(jnp.float32) * (2.0 * math.pi / SKY)
    return (jnp.cos(angles).astype(jnp.bfloat16), jnp.sin(angles).astype(jnp.bfloat16))


def grid_tables():
    counter = jnp.arange(SG, dtype=jnp.int32)
    angles = (counter[:, None] * counter[None, :] % SG).astype(jnp.float32) * (2.0 * math.pi / SG)
    return (jnp.cos(angles).astype(jnp.bfloat16), jnp.sin(angles).astype(jnp.bfloat16))


def contract_first(left, right):
    return lax.dot_general(
        left, right, (((0,), (0,)), ((), ())), preferred_element_type=jnp.float32
    )


def contract_last(left, right):
    return lax.dot_general(
        left, right, (((1,), (1,)), ((), ())), preferred_element_type=jnp.float32
    )


def shards(facet_image, row_offsets, col_offsets, vis_subgrid, vis_u, vis_v, observed):
    f32 = jnp.float32
    bf16 = jnp.bfloat16
    rows_count = lax.axis_size("frow")
    cols_count = lax.axis_size("fcol")
    facet_side = facet_image.shape[0]
    subgrids = NR * NC
    scale_in = 1.0 / (facet_side * math.sqrt(rows_count * cols_count))
    scale_out = 1.0 / (SG * math.sqrt(subgrids))
    row_pos = lax.axis_index("frow") * (SKY // rows_count) + jnp.arange(
        facet_side, dtype=jnp.int32
    ) * (SKY // (rows_count * facet_side))
    col_pos = lax.axis_index("fcol") * (SKY // cols_count) + jnp.arange(
        facet_side, dtype=jnp.int32
    ) * (SKY // (cols_count * facet_side))
    row_tabs = [
        jnp.concatenate(sky_tables(row_offsets[row_pick], row_pos), 0) for row_pick in range(NR)
    ]
    col_tabs = [
        jnp.concatenate(sky_tables(col_offsets[col_pick], col_pos), 0) for col_pick in range(NC)
    ]
    col_halves = [
        contract_last(facet_image, col_tabs[col_pick]).astype(bf16) for col_pick in range(NC)
    ]
    blocks_out = []
    for row_pick in range(NR):
        for col_pick in range(NC):
            product = jnp.dot(row_tabs[row_pick], col_halves[col_pick], preferred_element_type=f32)
            part_real = product[:SG, :SG] - product[SG:, SG:]
            part_imag = -(product[:SG, SG:] + product[SG:, :SG])
            blocks_out.append(jnp.concatenate([part_real, part_imag], 1) * scale_in)
    stacked = jnp.concatenate(blocks_out, 0)
    summed = lax.psum(stacked, ("frow", "fcol"))
    grid_bf = summed.astype(bf16)
    kcos, ksin = grid_tables()
    forward_block = jnp.concatenate(
        [jnp.concatenate([kcos, ksin], 1), jnp.concatenate([-ksin, kcos], 1)], 0
    )
    w_both = (
        jnp.dot(grid_bf, forward_block, preferred_element_type=f32)
        .astype(bf16)
        .reshape(subgrids, SG, 2 * SG)
    )
    with_cos = jnp.einsum("au,sav->suv", kcos, w_both, preferred_element_type=f32)
    with_sin = jnp.einsum("au,sav->suv", ksin, w_both, preferred_element_type=f32)
    hat_real = (with_cos[:, :, :SG] - with_sin[:, :, SG:]) / SG
    hat_imag = (with_sin[:, :, :SG] + with_cos[:, :, SG:]) / SG
    cell_ids = (vis_subgrid * SG + vis_u) * SG + vis_v
    model_vis = jnp.stack(
        [jnp.take(hat_real.reshape(-1), cell_ids), jnp.take(hat_imag.reshape(-1), cell_ids)]
    )
    residual = observed - model_vis
    cells_all = subgrids * SG * SG
    inverse_block = jnp.concatenate(
        [jnp.concatenate([kcos, -ksin], 1), jnp.concatenate([ksin, kcos], 1)], 0
    )
    local_real = jax.ops.segment_sum(residual[0], cell_ids, num_segments=cells_all)
    local_imag = jax.ops.segment_sum(residual[1], cell_ids, num_segments=cells_all)
    ghat_real, ghat_imag = lax.psum((local_real, local_imag), ("frow", "fcol"))
    ghat_both = jnp.concatenate(
        [
            ghat_real.reshape(subgrids * SG, SG).astype(bf16),
            ghat_imag.reshape(subgrids * SG, SG).astype(bf16),
        ],
        1,
    )
    v_flat = jnp.dot(ghat_both, inverse_block, preferred_element_type=f32).astype(bf16)
    v_both = v_flat.reshape(subgrids, SG, 2 * SG)
    back_cos = jnp.einsum("au,suv->sav", kcos, v_both, preferred_element_type=f32)
    back_sin = jnp.einsum("au,suv->sav", ksin, v_both, preferred_element_type=f32)
    back_real = ((back_cos[:, :, :SG] + back_sin[:, :, SG:]) / SG).astype(bf16)
    back_imag = ((back_cos[:, :, SG:] - back_sin[:, :, :SG]) / SG).astype(bf16)
    image = jnp.zeros((facet_side, facet_side), f32)
    for col_pick in range(NC):
        u_both = jnp.zeros((facet_side, 2 * SG), f32)
        for row_pick in range(NR):
            sub_index = row_pick * NC + col_pick
            g_real = back_real[sub_index]
            g_imag = back_imag[sub_index]
            right_side = jnp.concatenate(
                [jnp.concatenate([g_real, g_imag], 1), jnp.concatenate([-g_imag, g_real], 1)], 0
            )
            u_both = u_both + contract_first(row_tabs[row_pick], right_side)
        col_cos = col_tabs[col_pick][:SG]
        col_sin = col_tabs[col_pick][SG:]
        image = image + jnp.dot(
            u_both.astype(bf16), jnp.concatenate([col_cos, -col_sin], 0), preferred_element_type=f32
        )
    return (image * scale_out, residual)


def solution(mesh):
    in_specs = (
        P("frow", "fcol"),
        P(),
        P(),
        P(("frow", "fcol")),
        P(("frow", "fcol")),
        P(("frow", "fcol")),
        P(None, ("frow", "fcol")),
    )
    out_specs = (P("frow", "fcol"), P(None, ("frow", "fcol")))
    return jax.shard_map(shards, mesh=mesh, in_specs=in_specs, out_specs=out_specs, check_vma=False)
```

profile of v0, /device:TPU:0, one launch (start us, length us, event | category | flops | bytes accessed | tf_op | source)
XLA Modules:
  0.0 194.2 jit_solution(18069458550596602750)
XLA Ops:
  0.7 1.3 fusion.145
  3.3 4.6 %sine_convert_fusion.2 = (bf16[256,512]{1,0:T(8,128)(2,1)S(1)}, bf16[256,512]{1,0:T(8,128)(2,1)S(1)}, bf16[256,512]{1,0:T(8,128)(2,1)S(1)}, bf16[256,512]{1,0:T(8,128)(2,1)S(1)}) fusion(s32[512]{0:T(512)S(1)} %get-tuple-element.54, s32[256]{0:T(256)S(1)} %get-tuple-element.55, s32[512]{0:T(512)S(1)} %get-tuple-element.53, s32[256]{0:T(256)S(1)} %get-tuple-element.56, ...), kind=kLoop, calls=%fused_computation.116 | loop fusion | flops 4718592 | bytes 1056768 | tf_op jit(solution)/shard_map/convert_element_type | solution.py:22
  11.1 4.6 %cosine_convert_fusion.3 = (bf16[256,512]{1,0:T(8,128)(2,1)S(1)}, bf16[256,512]{1,0:T(8,128)(2,1)S(1)}, bf16[256,512]{1,0:T(8,128)(2,1)S(1)}, bf16[256,512]{1,0:T(8,128)(2,1)S(1)}) fusion(s32[512]{0:T(512)S(1)} %get-tuple-element.60, s32[256]{0:T(256)S(1)} %get-tuple-element.61, s32[512]{0:T(512)S(1)} %get-tuple-element.59, s32[256]{0:T(256)S(1)} %get-tuple-element.62, ...), kind=kLoop, calls=%fused_computation.123 | loop fusion | flops 4718592 | bytes 1056768 | tf_op jit(solution)/shard_map/convert_element_type | solution.py:22
  19.0 64.4 %all-reduce.3 = bf16[1024,512]{0,1:T(8,128)(2,1)} all-reduce(f32[1024,512]{0,1:T(8,128)S(1)} %pad_maximum_fusion), channel_id=1, replica_groups=mesh['frow'=4,'fcol'=8] {'frow','fcol'}, use_global_device_ids=true, to_apply=%region_0.1 | all-reduce | flops 524288 | bytes 3145728 | tf_op jit(solution)/shard_map/psum | solution.py:75
  83.4 1.1 sine_convert_fusion.4
  85.5 2.0 %convolution_convert_fusion.1 = bf16[1024,512]{1,0:T(8,128)(2,1)S(1)} fusion(bf16[1024,512]{0,1:T(8,128)(2,1)} %all-reduce.3, bf16[256,256]{1,0:T(8,128)(2,1)S(1)} %get-tuple-element.66, bf16[256,256]{1,0:T(8,128)(2,1)S(1)} %fusion.100, bf16[256,256]{1,0:T(8,128)(2,1)S(1)} %get-tuple-element.65), kind=kOutput, calls=%fused_computation.10 | convolution fusion | flops 539492352 | bytes 2490368 | tf_op jit(solution)/shard_map/dot_general | solution.py:82
  87.5 1.4 convolution_bitcast_fusion.2
  88.9 1.4 convolution_bitcast_fusion.3
  90.3 1.3 fusion.9
  93.3 4.3 %gather_fusion.1 = f32[512]{0:T(512)} fusion(f32[262144]{0:T(1024)S(1)} %bitcast.67, s32[1024]{0:T(1024)S(1)} %pad_clamp_fusion), kind=kCustom, calls=%fused_computation.1.clone | custom fusion | bytes 6144 | tf_op jit(solution)/shard_map/jit(_take)/gather | solution.py:92
  97.5 1.6 copy.15
  99.7 3.1 %gather_fusion = f32[512]{0:T(512)S(1)} fusion(f32[262144]{0:T(1024)S(1)} %bitcast.68, s32[1024]{0:T(1024)S(1)} %pad_clamp_fusion), kind=kCustom, calls=%fused_computation.clone | custom fusion | bytes 6144 | tf_op jit(solution)/shard_map/jit(_take)/gather | solution.py:92
  103.5 3.5 %scatter_custom_fusion = f32[262144]{0:T(1024)S(1)} fusion(s32[512]{0:T(512)S(1)} %copy-done.18, f32[512]{0:T(512)S(1)} %bitcast.78, f32[]{:T(128)} %constant.156.clone.1), kind=kCustom, calls=%fused_computation.120 | custom fusion | flops 512 | bytes 1048580 | tf_op jit(solution)/shard_map/scatter-add | solution.py:99
  107.0 3.7 %scatter_custom_fusion.1 = f32[262144]{0:T(1024)S(1)} fusion(s32[512]{0:T(512)} %get-tuple-element.6, f32[512]{0:T(512)} %bitcast.77, f32[]{:T(128)} %constant.156.clone.1), kind=kCustom, calls=%fused_computation.118 | custom fusion | flops 512 | bytes 1049088 | tf_op jit(solution)/shard_map/scatter-add | solution.py:100
  110.7 62.5 %all-reduce.4 = (bf16[262144]{0:T(1024)(128)(2,1)}, bf16[262144]{0:T(1024)(128)(2,1)}) all-reduce(f32[262144]{0:T(1024)S(1)} %scatter_custom_fusion.1, f32[262144]{0:T(1024)S(1)} %scatter_custom_fusion), channel_id=1, replica_groups=mesh['frow'=4,'fcol'=8] {'frow','fcol'}, use_global_device_ids=true, to_apply=%region_4.6 | all-reduce | flops 524288 | bytes 3145728 | tf_op jit(solution)/shard_map/psum | solution.py:101
  173.2 1.3 convert_element_type.148
  174.4 1.2 convert_element_type.150
  176.4 1.4 convolution_bitcast_fusion
  177.8 1.4 convolution_bitcast_fusion.1
  180.6 1.5 fusion.59
  182.0 1.5 fusion.36
  183.5 4.4 %fusion.138 = (bf16[256,512]{1,0:T(8,128)(2,1)S(1)}, bf16[256,512]{1,0:T(8,128)(2,1)S(1)}) fusion(s32[512]{0:T(512)S(1)} %get-tuple-element.54, s32[256]{0:T(256)S(1)} %copy-done.15, s32[512]{0:T(512)S(1)} %get-tuple-element.53, s32[256]{0:T(256)S(1)} %copy-done.17, s32[256]{0:T(256)S(1)} %get-tuple-element.55, s32[256]{0:T(256)S(1)} %copy-done.13), kind=kLoop, calls=%fused_computation.238 | loop fusion | flops 5242880 | bytes 532480 | tf_op jit(solution)/shard_map/neg | solution.py:129
  187.9 3.0 %fusion.3 = f32[512,512]{1,0:T(8,128)} fusion(f32[512,512]{1,0:T(8,128)} %fusion.36, bf16[256,512]{1,0:T(8,128)(2,1)S(1)} %copy-done.6, bf16[256,256]{0,1:T(8,128)(2,1)S(1)} %get-tuple-element.29, bf16[256,256]{0,1:T(8,128)(2,1)S(1)} %get-tuple-element.25, bf16[256,256]{0,1:T(8,128)(2,1)S(1)} %get-tuple-element.21, ...), kind=kOutput, calls=%fused_computation.19 | convolution fusion | flops 541589504 | bytes 3538944 | tf_op jit(solution)/shard_map/dot_general | solution.py:128
  190.9 3.3 %fusion = f32[512,512]{1,0:T(8,128)} fusion(f32[512,512]{1,0:T(8,128)} %fusion.3, f32[512,512]{1,0:T(8,128)} %fusion.59, bf16[256,512]{1,0:T(8,128)(2,1)S(1)} %copy-done.4, bf16[256,256]{0,1:T(8,128)(2,1)S(1)} %get-tuple-element.27, bf16[256,256]{0,1:T(8,128)(2,1)S(1)} %get-tuple-element.23, bf16[256,256]{0,1:T(8,128)(2,1)S(1)} %get-tuple-element.19, ...), kind=kOutput, calls=%fused_computation.12 | convolution fusion | flops 542113792 | bytes 4587520 | tf_op jit(solution)/shard_map/dot_general | solution.py:128
  (86 shorter events, 13.3 us)
Async XLA Ops:
  0.6 8.1 %copy-start = (bf16[512,512]{1,0:T(8,128)(2,1)S(1)}, bf16[512,512]{1,0:T(8,128)(2,1)}, u32[]{:S(2)}) copy-start(bf16[512,512]{1,0:T(8,128)(2,1)} %param.9) | copy-start | bytes 1572868
  0.6 8.5 %copy-start.24 = (s32[2]{0:T(128)S(1)}, s32[2]{0:T(128)}, u32[]{:S(2)}) copy-start(s32[2]{0:T(128)} %param.10) | copy-start | bytes 28
  2.7 13.6 %copy-start.12 = (s32[256]{0:T(256)}, s32[256]{0:T(256)S(1)}, u32[]{:S(2)}) copy-start(s32[256]{0:T(256)S(1)} %get-tuple-element.56) | copy-start | bytes 3076
  3.3 12.9 %copy-start.14 = (s32[256]{0:T(256)}, s32[256]{0:T(256)S(1)}, u32[]{:S(2)}) copy-start(s32[256]{0:T(256)S(1)} %get-tuple-element.57) | copy-start | bytes 3076
  3.3 12.9 %copy-start.16 = (s32[256]{0:T(256)}, s32[256]{0:T(256)S(1)}, u32[]{:S(2)}) copy-start(s32[256]{0:T(256)S(1)} %get-tuple-element.58) | copy-start | bytes 3076
  8.0 0.7 copy-start.5
  8.0 8.4 %copy-start.3 = (bf16[256,512]{1,0:T(8,128)(2,1)}, bf16[256,512]{1,0:T(8,128)(2,1)S(1)}, u32[]{:S(2)}) copy-start(bf16[256,512]{1,0:T(8,128)(2,1)S(1)} %get-tuple-element.45) | copy-start | bytes 786436
  15.7 1.1 copy-start.1
  84.5 3.0 %copy-start.7 = (bf16[256,256]{1,0:T(8,128)(2,1)}, bf16[256,256]{1,0:T(8,128)(2,1)S(1)}, u32[]{:S(2)}) copy-start(bf16[256,256]{1,0:T(8,128)(2,1)S(1)} %get-tuple-element.66) | copy-start | bytes 393220
  85.5 2.0 %copy-start.9 = (bf16[256,256]{1,0:T(8,128)(2,1)}, bf16[256,256]{1,0:T(8,128)(2,1)S(1)}, u32[]{:S(2)}) copy-start(bf16[256,256]{1,0:T(8,128)(2,1)S(1)} %fusion.100) | copy-start | bytes 393220
  91.6 0.9 copy-start.21
  92.0 0.7 copy-start.23
  99.6 3.2 %copy-start.18 = (s32[512]{0:T(512)S(1)}, s32[512]{0:T(512)}, u32[]{:S(2)}) copy-start(s32[512]{0:T(512)} %get-tuple-element.6) | copy-start | bytes 6148
  99.6 3.2 %copy-start.19 = (f32[512]{0:T(512)S(1)}, f32[512]{0:T(512)}, u32[]{:S(2)}) copy-start(f32[512]{0:T(512)} %gather_fusion.1) | copy-start | bytes 6148
  99.7 3.2 %copy-start.20 = (f32[2,512]{1,0:T(2,128)S(1)}, f32[2,512]{1,0:T(2,128)}, u32[]{:S(2)}) copy-start(f32[2,512]{1,0:T(2,128)} %param.15) | copy-start | bytes 12292
  102.9 70.3 %copy-start.11 = (f32[2,512]{1,0:T(2,128)}, f32[2,512]{1,0:T(2,128)S(1)}, u32[]{:S(2)}) copy-start(f32[2,512]{1,0:T(2,128)S(1)} %maximum_subtract_fusion) | copy-start | bytes 12292
  173.2 2.5 %copy-start.8 = (bf16[256,256]{1,0:T(8,128)(2,1)S(1)}, bf16[256,256]{1,0:T(8,128)(2,1)}, u32[]{:S(2)}) copy-start(bf16[256,256]{1,0:T(8,128)(2,1)} %copy-done.7) | copy-start | bytes 393220
  173.2 2.5 %copy-start.10 = (bf16[256,256]{1,0:T(8,128)(2,1)S(1)}, bf16[256,256]{1,0:T(8,128)(2,1)}, u32[]{:S(2)}) copy-start(bf16[256,256]{1,0:T(8,128)(2,1)} %copy-done.9) | copy-start | bytes 393220
  179.6 1.0 copy-start.2
  182.0 1.5 copy-start.13
  182.0 1.5 copy-start.15
  182.0 1.5 copy-start.17
  182.0 5.8 %copy-start.6 = (bf16[256,512]{1,0:T(8,128)(2,1)S(1)}, bf16[256,512]{1,0:T(8,128)(2,1)}, u32[]{:S(2)}) copy-start(bf16[256,512]{1,0:T(8,128)(2,1)} %copy-done.5) | copy-start | bytes 786436
  187.9 3.0 %copy-start.4 = (bf16[256,512]{1,0:T(8,128)(2,1)S(1)}, bf16[256,512]{1,0:T(8,128)(2,1)}, u32[]{:S(2)}) copy-start(bf16[256,512]{1,0:T(8,128)(2,1)} %copy-done.3) | copy-start | bytes 786436
  (1 other events, 0.7 us)
where the time goes:
time: 195 us; the launch traced here: 194 us
  blocking collectives  127 us (65%)
  other arithmetic  28.6 us (15%)
  matrix products  20.3 us (10%)
  local copies, waits for them, and re-layouts  17.1 us (9%)
    psum x1, blocking collectives, shards(): summed = lax.psum(stacked, ('frow', 'fcol'))  64.4 us
    psum x1, blocking collectives, shards(): ghat_real, ghat_imag = lax.psum((local_real, local_imag), ('frow', 'fcol'))  62.5 us
    dot_general x2, matrix products, shards(): jnp.dot(u_both.astype(bf16), jnp.concatenate([col_cos, -col_sin], 0), pre...  6.29 us
    convert_element_type x1, other arithmetic, sky_tables(): jnp.sin(angles).astype(jnp.bfloat16)  4.64 us
    convert_element_type x1, other arithmetic, sky_tables(): jnp.cos(angles).astype(jnp.bfloat16)  4.64 us
    neg x1, other arithmetic, shards(): -col_sin  4.36 us
    gather x1, local copies, waits for them, and re-layouts, shards(): jnp.take(hat_imag.reshape(-1), cell_ids)  4.27 us

commit v1 on v0

--- a/solution.py
+++ b/solution.py
@@ -8,6 +8,11 @@
 SG = 256
 NR = 2
 NC = 2
+
+
+def axis_by_axis(value, one, other):
+    inner = lax.psum(value, one)
+    return lax.psum(inner, other)
 
 
 def wrapped(frequency, position):
@@ -98,7 +103,7 @@
     )
     local_real = jax.ops.segment_sum(residual[0], cell_ids, num_segments=cells_all)
     local_imag = jax.ops.segment_sum(residual[1], cell_ids, num_segments=cells_all)
-    ghat_real, ghat_imag = lax.psum((local_real, local_imag), ("frow", "fcol"))
+    ghat_real, ghat_imag = axis_by_axis((local_real, local_imag), "fcol", "frow")
     ghat_both = jnp.concatenate(
         [
             ghat_real.reshape(subgrids * SG, SG).astype(bf16),

time: 195 us -> 287 us (1.47)
  waiting for transfers between devices: 0 us -> 96.8 us
  blocking collectives: 127 us -> 106 us
  between operations: 1.22 us -> 14.6 us
    psum x0 -> x1, waiting for transfers between devices: none -> 96.8 us  [axis_by_axis(): inner = lax.psum(value, one)]
    psum x1, blocking collectives: 62.5 us -> 41.3 us  [axis_by_axis(): return lax.psum(inner, other)]
  transfers between devices with their start and end apart: 0 -> 1, of which waited for: 0 -> 1; matrix products, arithmetic and copies ran while one was open for 0% -> 2% of each run, Pallas kernels for 0% -> 0%
where the time goes in v1:
time: 287 us
  blocking collectives  106 us (37%)
  waiting for transfers between devices  96.8 us (34%)
  other arithmetic  31.3 us (11%)
  matrix products  21.3 us (7%)
  local copies, waits for them, and re-layouts  16.9 us (6%)
  between operations  14.6 us (5%)
    psum x1, waiting for transfers between devices, axis_by_axis(): inner = lax.psum(value, one)  96.8 us
    psum x1, blocking collectives, shards(): summed = lax.psum(stacked, ('frow', 'fcol'))  64.4 us
    psum x1, blocking collectives, axis_by_axis(): return lax.psum(inner, other)  41.3 us
    dot_general x2, matrix products, shards(): jnp.dot(u_both.astype(bf16), jnp.concatenate([col_cos, -col_sin], 0), pre...  6.26 us
  transfers between devices with their start and end apart: 1, of which 1 were waited for; matrix products, arithmetic and copies ran while one was open for 2% of the time, Pallas kernels for 0%

profile of v1, /device:TPU:0, one launch (start us, length us, event | category | flops | bytes accessed | tf_op | source)
XLA Modules:
  0.0 286.5 jit_solution(15744373363774511993)
XLA Ops:
  12.6 4.6 %sine_convert_fusion.2 = (bf16[256,512]{1,0:T(8,128)(2,1)S(1)}, bf16[256,512]{1,0:T(8,128)(2,1)S(1)}, bf16[256,512]{1,0:T(8,128)(2,1)S(1)}, bf16[256,512]{1,0:T(8,128)(2,1)S(1)}) fusion(s32[512]{0:T(512)S(1)} %get-tuple-element.56, s32[256]{0:T(256)S(1)} %get-tuple-element.57, s32[512]{0:T(512)S(1)} %get-tuple-element.55, s32[256]{0:T(256)S(1)} %get-tuple-element.58, ...), kind=kLoop, calls=%fused_computation.116 | loop fusion | flops 4718592 | bytes 1056768 | tf_op jit(solution)/shard_map/convert_element_type | solution.py:27
  18.4 4.6 %cosine_convert_fusion.3 = (bf16[256,512]{1,0:T(8,128)(2,1)S(1)}, bf16[256,512]{1,0:T(8,128)(2,1)S(1)}, bf16[256,512]{1,0:T(8,128)(2,1)S(1)}, bf16[256,512]{1,0:T(8,128)(2,1)S(1)}) fusion(s32[512]{0:T(512)S(1)} %get-tuple-element.62, s32[256]{0:T(256)S(1)} %get-tuple-element.63, s32[512]{0:T(512)S(1)} %get-tuple-element.61, s32[256]{0:T(256)S(1)} %get-tuple-element.64, ...), kind=kLoop, calls=%fused_computation.123 | loop fusion | flops 4718592 | bytes 1056768 | tf_op jit(solution)/shard_map/convert_element_type | solution.py:27
  25.0 1.7 sine_convert_fusion.4
  26.7 1.6 fusion.100
  29.1 64.4 %all-reduce.7 = bf16[1024,512]{0,1:T(8,128)(2,1)} all-reduce(f32[1024,512]{0,1:T(8,128)S(1)} %pad_maximum_fusion), channel_id=1, replica_groups=mesh['frow'=4,'fcol'=8] {'frow','fcol'}, use_global_device_ids=true, to_apply=%region_0.1 | all-reduce | flops 524288 | bytes 3145728 | tf_op jit(solution)/shard_map/psum | solution.py:80
  93.6 2.0 convolution_convert_fusion.1
  95.6 1.4 convolution_bitcast_fusion.2
  97.0 1.4 convolution_bitcast_fusion.3
  101.3 2.5 copy.15
  103.9 1.8 copy.23
  105.7 4.3 %gather_fusion.1 = f32[512]{0:T(512)} fusion(f32[262144]{0:T(1024)S(1)} %bitcast.67, s32[1024]{0:T(1024)S(1)} %pad_clamp_fusion), kind=kCustom, calls=%fused_computation.1.clone | custom fusion | bytes 6144 | tf_op jit(solution)/shard_map/jit(_take)/gather | solution.py:97
  109.9 3.1 %gather_fusion = f32[512]{0:T(512)S(1)} fusion(f32[262144]{0:T(1024)S(1)} %bitcast.68, s32[1024]{0:T(1024)S(1)} %pad_clamp_fusion), kind=kCustom, calls=%fused_computation.clone | custom fusion | bytes 6144 | tf_op jit(solution)/shard_map/jit(_take)/gather | solution.py:97
  113.2 4.3 %scatter_custom_fusion = f32[262144]{0:T(1024)} fusion(s32[512]{0:T(512)S(1)} %copy-done.14, f32[512]{0:T(512)S(1)} %bitcast.78, f32[]{:T(128)} %constant.156.clone.1), kind=kCustom, calls=%fused_computation.120 | custom fusion | flops 512 | bytes 1048580 | tf_op jit(solution)/shard_map/scatter-add | solution.py:104
  117.5 4.2 %scatter_custom_fusion.1 = f32[262144]{0:T(1024)} fusion(s32[512]{0:T(512)S(1)} %copy-done.14, f32[512]{0:T(512)S(1)} %bitcast.77, f32[]{:T(128)} %constant.156.clone.1), kind=kCustom, calls=%fused_computation.118 | custom fusion | flops 512 | bytes 1048580 | tf_op jit(solution)/shard_map/scatter-add | solution.py:105
  121.8 4.4 %fusion.138 = (bf16[256,512]{1,0:T(8,128)(2,1)S(1)}, bf16[256,512]{1,0:T(8,128)(2,1)S(1)}) fusion(s32[512]{0:T(512)S(1)} %get-tuple-element.56, s32[256]{0:T(256)S(1)} %copy-done.11, s32[512]{0:T(512)S(1)} %get-tuple-element.55, s32[256]{0:T(256)S(1)} %copy-done.13, s32[256]{0:T(256)S(1)} %get-tuple-element.57, s32[256]{0:T(256)S(1)} %copy-done.9), kind=kLoop, calls=%fused_computation.238 | loop fusion | flops 5242880 | bytes 532480 | tf_op jit(solution)/shard_map/neg | solution.py:134
  126.2 96.8 %all-reduce.6.cloned.1.call-done = (f32[262144]{0:T(1024)}, f32[262144]{0:T(1024)}) async-done(((f32[262144]{0:T(1024)}, f32[262144]{0:T(1024)}), (f32[262144]{0:T(1024)}, f32[262144]{0:T(1024)})) %all-reduce.6.cloned.1.call-update) | async-done | bytes 2097168 | tf_op jit(solution)/shard_map/psum | solution.py:14
  222.9 41.3 %all-reduce.8 = (bf16[262144]{0:T(1024)(128)(2,1)S(1)}, bf16[262144]{0:T(1024)(128)(2,1)S(1)}) all-reduce(f32[262144]{0:T(1024)} %get-tuple-element.3, f32[262144]{0:T(1024)} %get-tuple-element.4), channel_id=1, replica_groups=mesh['frow'=4,'fcol'=8] {'frow'}, use_global_device_ids=true, to_apply=%region_6.8 | all-reduce | flops 524288 | bytes 3145728 | tf_op jit(solution)/shard_map/psum | solution.py:15
  264.6 1.7 convolution_convert_fusion
  266.3 1.4 convolution_bitcast_fusion
  267.7 1.4 convolution_bitcast_fusion.1
  270.5 1.5 fusion.59
  272.0 1.5 fusion.36
  273.4 3.0 %fusion.3 = f32[512,512]{1,0:T(8,128)} fusion(f32[512,512]{1,0:T(8,128)} %fusion.36, bf16[256,512]{1,0:T(8,128)(2,1)S(1)} %copy-done.6, bf16[256,256]{0,1:T(8,128)(2,1)S(1)} %get-tuple-element.31, bf16[256,256]{0,1:T(8,128)(2,1)S(1)} %get-tuple-element.27, bf16[256,256]{0,1:T(8,128)(2,1)S(1)} %get-tuple-element.23, ...), kind=kOutput, calls=%fused_computation.19 | convolution fusion | flops 541589504 | bytes 3538944 | tf_op jit(solution)/shard_map/dot_general | solution.py:133
  276.4 3.3 %fusion = f32[512,512]{1,0:T(8,128)} fusion(f32[512,512]{1,0:T(8,128)} %fusion.3, f32[512,512]{1,0:T(8,128)} %fusion.59, bf16[256,512]{1,0:T(8,128)(2,1)S(1)} %copy-done.4, bf16[256,256]{0,1:T(8,128)(2,1)S(1)} %get-tuple-element.29, bf16[256,256]{0,1:T(8,128)(2,1)S(1)} %get-tuple-element.25, bf16[256,256]{0,1:T(8,128)(2,1)S(1)} %get-tuple-element.21, ...), kind=kOutput, calls=%fused_computation.12 | convolution fusion | flops 542113792 | bytes 4587520 | tf_op jit(solution)/shard_map/dot_general | solution.py:133
  (79 shorter events, 13.7 us)
Async XLA Ops:
  7.2 10.1 %copy-start = (bf16[512,512]{1,0:T(8,128)(2,1)S(1)}, bf16[512,512]{1,0:T(8,128)(2,1)}, u32[]{:S(2)}) copy-start(bf16[512,512]{1,0:T(8,128)(2,1)} %param.9) | copy-start | bytes 1572868
  7.2 215.7 %all-reduce.6.cloned.1.call-start = ((), (), s32[]{:S(2)}) async-start(), calls=%async_computation | async-start | bytes 4194304 | tf_op jit(solution)/shard_map/psum | solution.py:14
  9.2 9.2 %copy-start.8 = (s32[256]{0:T(256)}, s32[256]{0:T(256)S(1)}, u32[]{:S(2)}) copy-start(s32[256]{0:T(256)S(1)} %get-tuple-element.58) | copy-start | bytes 3076
  9.9 8.5 %copy-start.10 = (s32[256]{0:T(256)}, s32[256]{0:T(256)S(1)}, u32[]{:S(2)}) copy-start(s32[256]{0:T(256)S(1)} %get-tuple-element.59) | copy-start | bytes 3076
  9.9 8.5 %copy-start.12 = (s32[256]{0:T(256)}, s32[256]{0:T(256)S(1)}, u32[]{:S(2)}) copy-start(s32[256]{0:T(256)S(1)} %get-tuple-element.60) | copy-start | bytes 3076
  17.2 0.7 copy-start.5
  17.2 5.8 %copy-start.3 = (bf16[256,512]{1,0:T(8,128)(2,1)}, bf16[256,512]{1,0:T(8,128)(2,1)S(1)}, u32[]{:S(2)}) copy-start(bf16[256,512]{1,0:T(8,128)(2,1)S(1)} %get-tuple-element.47) | copy-start | bytes 786436
  23.1 1.0 copy-start.1
  99.7 0.9 copy-start.17
  100.1 0.7 copy-start.18
  100.1 0.7 copy-start.19
  109.9 3.2 %copy-start.14 = (s32[512]{0:T(512)S(1)}, s32[512]{0:T(512)}, u32[]{:S(2)}) copy-start(s32[512]{0:T(512)} %get-tuple-element.8) | copy-start | bytes 6148
  109.9 3.2 %copy-start.15 = (f32[512]{0:T(512)S(1)}, f32[512]{0:T(512)}, u32[]{:S(2)}) copy-start(f32[512]{0:T(512)} %gather_fusion.1) | copy-start | bytes 6148
  109.9 3.2 %copy-start.16 = (f32[2,512]{1,0:T(2,128)S(1)}, f32[2,512]{1,0:T(2,128)}, u32[]{:S(2)}) copy-start(f32[2,512]{1,0:T(2,128)} %param.15) | copy-start | bytes 12292
  113.1 8.6 %copy-start.7 = (f32[2,512]{1,0:T(2,128)}, f32[2,512]{1,0:T(2,128)S(1)}, u32[]{:S(2)}) copy-start(f32[2,512]{1,0:T(2,128)S(1)} %maximum_subtract_fusion) | copy-start | bytes 12292
  113.2 8.6 %copy-start.9 = (s32[256]{0:T(256)S(1)}, s32[256]{0:T(256)}, u32[]{:S(2)}) copy-start(s32[256]{0:T(256)} %copy-done.8) | copy-start | bytes 3076
  113.2 8.6 %copy-start.11 = (s32[256]{0:T(256)S(1)}, s32[256]{0:T(256)}, u32[]{:S(2)}) copy-start(s32[256]{0:T(256)} %copy-done.10) | copy-start | bytes 3076
  113.2 8.6 %copy-start.13 = (s32[256]{0:T(256)S(1)}, s32[256]{0:T(256)}, u32[]{:S(2)}) copy-start(s32[256]{0:T(256)} %copy-done.12) | copy-start | bytes 3076
  269.6 1.0 copy-start.2
  272.0 1.5 copy-start.6
  273.4 3.0 %copy-start.4 = (bf16[256,512]{1,0:T(8,128)(2,1)S(1)}, bf16[256,512]{1,0:T(8,128)(2,1)}, u32[]{:S(2)}) copy-start(bf16[256,512]{1,0:T(8,128)(2,1)} %copy-done.3) | copy-start | bytes 786436
Sparse Core Ops, SparseCore 0:
  121.9 101.0 all-reduce.5
